TPU v7x, 32 devices: a whole 2x2x4 slice. The times are simulated.
32 devices in a mesh: cells: 16 (over z, y, x), feat: 2 (over core).
Axes of the slice: x: 2, y: 2, z: 4, core: 2. Of those that a mesh axis runs over, the one named last changes fastest.
Arguments:
- features: float32 [32768, 4096], P('cells', 'feat'), may hold values from -6 to 6
- labels: int32 [32768], P('cells'), may hold values from 0 to 7
- weights: float32 [8, 4096], P(None, 'feat'), may hold values from -0.09375 to 0.09375
Outputs:
- new_weights: float32 [8, 4096], P(None, 'feat')
- new_logits: float32 [8, 32768], P(None, 'cells')
All inputs are finite; a program needn't handle non-finite values.
Results may differ from a plain program's by a relative error of at most 0.00018.
Values sent between devices are 32-bit elements; how exact they have to be, the bound alone decides.
A program may use at most 64 MiB of HBM per device.

v0:
```python
import jax
import jax.numpy as jnp
from jax import lax
from jax.sharding import PartitionSpec as P

ITERS = 2
HIGH = lax.Precision.HIGHEST
RIDGE = 0.01


def on_device(features, labels, weights):
    rows = features.shape[0]
    classes = weights.shape[0]
    count = rows * lax.axis_size("cells") * 1.0

    def row_sums(coeffs):
        local_rows = lax.dot_general(
            coeffs,
            features,
            (((1,), (1,)), ((), ())),
            precision=HIGH,
            preferred_element_type=jnp.float32,
        )
        summed = lax.psum(local_rows, "feat")
        return (summed, summed[classes:])

    def collect(terms):
        return lax.psum(jnp.dot(terms, features, precision=HIGH), "cells")

    def total(packed):
        return lax.psum(packed, "feat")

    def inner(left, right):
        return total(jnp.sum(left * right))

    logits, unused = row_sums(weights)
    expo = jnp.exp(logits)
    probs = expo / jnp.sum(expo, axis=0, keepdims=True)
    onehot = (labels[None, :] == jnp.arange(classes, dtype=jnp.int32)[:, None]).astype(jnp.float32)
    grad = collect(probs - onehot) / count + RIDGE * weights
    resid = -grad
    direction = resid
    rr_now = jnp.float32(0.0)
    rr_now = inner(resid, resid)
    step = jnp.zeros_like(weights)
    moved = jnp.zeros_like(logits)
    for it in range(ITERS):
        full_direction = direction
        image, unused = row_sums(full_direction)
        curv = probs * image - probs * jnp.sum(probs * image, axis=0, keepdims=True)
        product = collect(curv) / count + RIDGE * direction
        alpha = rr_now / inner(direction, product)
        step = step + alpha * direction
        moved = moved + alpha * image
        resid = resid - alpha * product
        if it + 1 < ITERS:
            rr_next = inner(resid, resid)
            direction = resid + rr_next / rr_now * direction
            rr_now = rr_next
    return (weights + step, logits + moved)


def solution(mesh):
    return jax.shard_map(
        on_device,
        mesh=mesh,
        in_specs=(P("cells", "feat"), P("cells"), P(None, "feat")),
        out_specs=(P(None, "feat"), P(None, "cells")),
        check_vma=False,
    )
```

profile of v0, /device:TPU:0, one launch (start us, length us, event | category | flops | bytes accessed | tf_op | source)
XLA Modules:
  0.0 500.8 jit_solution(12203118077418781199)
XLA Ops:
  7.2 0.0 all-reduce.8.cloned.1.call-start
  7.2 19.7 %fusion.21 = f32[8,2048]{1,0:T(8,128)} fusion(f32[8,2048]{1,0:T(8,128)} %param.5, f32[2048,2048]{1,0:T(8,128)} %param.3), kind=kOutput, calls=%fused_computation.32 | convolution fusion | flops 402653184 | bytes 16908288 | tf_op jit(solution)/shard_map/dot_general | solution.py:17
  26.9 0.0 all-reduce.8.cloned.1.call-update
  27.0 0.0 all-reduce.10.cloned.1.call-start
  27.0 20.5 %all-reduce.8.cloned.1.call-done = f32[8,2048]{1,0:T(8,128)} async-done(((f32[8,2048]{1,0:T(8,128)}), f32[8,2048]{1,0:T(8,128)}) %all-reduce.8.cloned.1.call-update) | async-done | bytes 65552 | tf_op jit(solution)/shard_map/psum | solution.py:24
  47.6 0.9 exponential_reduce_fusion
  48.5 14.2 %fusion.6 = f32[8,2048]{1,0:T(8,128)} fusion(f32[2048,2048]{1,0:T(8,128)} %param.3, s32[2048]{0:T(1024)S(1)} %copy-done.5, f32[8,2048]{1,0:T(8,128)} %all-reduce.8.cloned.1.call-done, f32[2048]{0:T(1024)S(1)} %exponential_reduce_fusion), kind=kOutput, calls=%fused_computation.16 | convolution fusion | flops 402718720 | bytes 16924672 | tf_op jit(solution)/shard_map/dot_general | solution.py:28
  62.6 0.0 all-reduce.10.cloned.1.call-update
  62.6 0.2 all-reduce.12.cloned.1.call-start
  62.9 104.6 %all-reduce.10.cloned.1.call-done = f32[8,2048]{1,0:T(8,128)} async-done(((f32[8,2048]{1,0:T(8,128)}), f32[8,2048]{1,0:T(8,128)}) %all-reduce.10.cloned.1.call-update) | async-done | bytes 65552 | tf_op jit(solution)/shard_map/psum | solution.py:28
  167.5 0.9 multiply_add_fusion.2
  168.3 17.7 %fusion.9 = f32[8,2048]{1,0:T(8,128)} fusion(f32[2048,2048]{1,0:T(8,128)} %param.3, f32[8,2048]{1,0:T(8,128)S(1)} %multiply_add_fusion.2), kind=kOutput, calls=%fused_computation.22 | convolution fusion | flops 402669568 | bytes 16908288 | tf_op jit(solution)/shard_map/dot_general | solution.py:17
  186.0 0.0 all-reduce.14.cloned.1.call-start
  186.1 16.9 %all-reduce.12.cloned.1.call-done = f32[8,2048]{1,0:T(8,128)} async-done(((f32[8,2048]{1,0:T(8,128)}), f32[8,2048]{1,0:T(8,128)}) %all-reduce.12.cloned.1.call-update) | async-done | bytes 65552 | tf_op jit(solution)/shard_map/psum | solution.py:24
  202.9 0.9 fusion.18
  203.8 12.1 %fusion.3 = f32[8,2048]{1,0:T(8,128)} fusion(f32[2048,2048]{1,0:T(8,128)} %param.3, f32[2048]{0:T(1024)S(1)} %fusion.18, f32[8,2048]{1,0:T(8,128)S(1)} %copy-done, f32[2048]{0:T(1024)S(1)} %exponential_reduce_fusion, f32[8,2048]{1,0:T(8,128)} %all-reduce.12.cloned.1.call-done), kind=kOutput, calls=%fused_computation.11 | convolution fusion | flops 402718720 | bytes 16990208 | tf_op jit(solution)/shard_map/dot_general | solution.py:28
  215.9 0.0 all-reduce.14.cloned.1.call-update
  215.9 0.0 all-reduce.16.cloned.1.call-start
  216.0 104.8 %all-reduce.14.cloned.1.call-done = f32[8,2048]{1,0:T(8,128)} async-done(((f32[8,2048]{1,0:T(8,128)}), f32[8,2048]{1,0:T(8,128)}) %all-reduce.14.cloned.1.call-update) | async-done | bytes 65552 | tf_op jit(solution)/shard_map/psum | solution.py:28
  320.8 1.5 multiply_reduce_fusion.2
  322.2 3.1 all-reduce
  326.6 1.5 multiply_reduce_fusion.1
  328.1 3.4 psum.76
  332.8 19.8 %fusion.14 = f32[8,2048]{1,0:T(8,128)} fusion(f32[2048,2048]{1,0:T(8,128)} %param.3, f32[8,2048]{1,0:T(8,128)S(1)} %multiply_add_fusion.2, f32[8,2048]{1,0:T(8,128)} %all-reduce.14.cloned.1.call-done, f32[]{:T(128)S(6)} %div.31, f32[]{:T(128)S(6)} %div.30), kind=kOutput, calls=%fused_computation.27 | convolution fusion | flops 402784256 | bytes 16973832 | tf_op jit(solution)/shard_map/dot_general | solution.py:17
  352.6 0.0 all-reduce.18.cloned.1.call-start
  352.6 16.9 %all-reduce.16.cloned.1.call-done = f32[8,2048]{1,0:T(8,128)} async-done(((f32[8,2048]{1,0:T(8,128)}), f32[8,2048]{1,0:T(8,128)}) %all-reduce.16.cloned.1.call-update) | async-done | bytes 65552 | tf_op jit(solution)/shard_map/psum | solution.py:24
  369.5 0.9 fusion.20
  370.5 12.1 %fusion = f32[8,2048]{1,0:T(8,128)} fusion(f32[2048,2048]{1,0:T(8,128)} %param.3, f32[2048]{0:T(1024)S(1)} %fusion.20, f32[8,2048]{1,0:T(8,128)S(1)} %copy-done, f32[2048]{0:T(1024)S(1)} %exponential_reduce_fusion, f32[8,2048]{1,0:T(8,128)} %all-reduce.16.cloned.1.call-done), kind=kOutput, calls=%fused_computation.3 | convolution fusion | flops 402718720 | bytes 16990208 | tf_op jit(solution)/shard_map/dot_general | solution.py:28
  382.6 104.8 %all-reduce.18.cloned.1.call-done = f32[8,2048]{1,0:T(8,128)} async-done(((f32[8,2048]{1,0:T(8,128)}), f32[8,2048]{1,0:T(8,128)}) %all-reduce.18.cloned.1.call-update) | async-done | bytes 65552 | tf_op jit(solution)/shard_map/psum | solution.py:28
  487.4 1.5 multiply_reduce_fusion
  488.9 3.1 psum.79
  493.3 0.7 add_add_fusion
  (15 shorter events, 0.1 us)
Async XLA Ops:
  7.2 160.3 %copy-start.2 = (f32[8,2048]{1,0:T(8,128)S(1)}, f32[8,2048]{1,0:T(8,128)}, u32[]{:S(2)}) copy-start(f32[8,2048]{1,0:T(8,128)} %param.5) | copy-start | bytes 196612
  7.2 41.3 %copy-start.5 = (s32[2048]{0:T(1024)S(1)}, s32[2048]{0:T(1024)}, u32[]{:S(2)}) copy-start(s32[2048]{0:T(1024)} %param.4) | copy-start | bytes 24580
  7.2 40.4 %all-reduce.8.cloned.1.call-start = ((), (), s32[]{:S(2)}) async-start(), calls=%async_computation | async-start | bytes 131072 | tf_op jit(solution)/shard_map/psum | solution.py:24
  27.0 140.5 %all-reduce.10.cloned.1.call-start = ((), (), s32[]{:S(2)}) async-start(), calls=%async_computation.1 | async-start | bytes 131072 | tf_op jit(solution)/shard_map/psum | solution.py:28
  48.4 154.5 %copy-start = (f32[8,2048]{1,0:T(8,128)S(1)}, f32[8,2048]{1,0:T(8,128)}, u32[]{:S(2)}) copy-start(f32[8,2048]{1,0:T(8,128)} %all-reduce.8.cloned.1.call-done) | copy-start | bytes 196612
  62.6 140.3 %all-reduce.12.cloned.1.call-start = ((), (), s32[]{:S(2)}) async-start(), calls=%async_computation.2 | async-start | bytes 131072 | tf_op jit(solution)/shard_map/psum | solution.py:24
  186.0 134.7 %all-reduce.14.cloned.1.call-start = ((), (), s32[]{:S(2)}) async-start(), calls=%async_computation.3 | async-start | bytes 131072 | tf_op jit(solution)/shard_map/psum | solution.py:28
  215.9 153.6 %all-reduce.16.cloned.1.call-start = ((), (), s32[]{:S(2)}) async-start(), calls=%async_computation.4 | async-start | bytes 131072 | tf_op jit(solution)/shard_map/psum | solution.py:24
  332.8 154.6 %copy-start.1 = (f32[8,2048]{1,0:T(8,128)S(1)}, f32[8,2048]{1,0:T(8,128)}, u32[]{:S(2)}) copy-start(f32[8,2048]{1,0:T(8,128)} %all-reduce.14.cloned.1.call-done) | copy-start | bytes 196612
  332.8 160.5 %copy-start.3 = (f32[8,2048]{1,0:T(8,128)S(1)}, f32[8,2048]{1,0:T(8,128)}, u32[]{:S(2)}) copy-start(f32[8,2048]{1,0:T(8,128)} %all-reduce.12.cloned.1.call-done) | copy-start | bytes 196612
  352.6 134.8 %all-reduce.18.cloned.1.call-start = ((), (), s32[]{:S(2)}) async-start(), calls=%async_computation.5 | async-start | bytes 131072 | tf_op jit(solution)/shard_map/psum | solution.py:28
  369.5 123.8 %copy-start.4 = (f32[8,2048]{1,0:T(8,128)S(1)}, f32[8,2048]{1,0:T(8,128)}, u32[]{:S(2)}) copy-start(f32[8,2048]{1,0:T(8,128)} %all-reduce.16.cloned.1.call-done) | copy-start | bytes 196612
Sparse Core Ops, SparseCore 0:
  27.1 20.4 all-reduce.7
  62.8 104.6 all-reduce.9
  186.1 16.7 all-reduce.11
  216.0 104.6 all-reduce.13
  352.7 16.7 all-reduce.15
  382.7 104.6 all-reduce.17
where the time goes:
time: 501 us
  waiting for transfers between devices  369 us (74%)
  matrix products  95.5 us (19%)
  between operations  18.2 us (4%)
  blocking collectives  9.52 us (2%)
  other arithmetic  8.63 us (2%)
    psum x3, waiting for transfers between devices, collect(): return lax.psum(jnp.dot(terms, features, precision=HIGH), 'cells')  314 us
    dot_general x3, matrix products, row_sums(): lax.dot_general(coeffs, features, (((1,), (1,)), ((), ())), precision=HIG...  57.1 us
    psum x3, waiting for transfers between devices, row_sums(): summed = lax.psum(local_rows, 'feat')  54.3 us
    dot_general x3, matrix products, collect(): return lax.psum(jnp.dot(terms, features, precision=HIGH), 'cells')  38.3 us
  transfers between devices with their start and end apart: 6, of which 6 were waited for; matrix products, arithmetic and copies ran while one was open for 0% of the time, Pallas kernels for 0%

commit v1 on v0

--- a/solution.py
+++ b/solution.py
@@ -25,7 +25,7 @@
         return (summed, summed[classes:])
 
     def collect(terms):
-        return lax.psum(jnp.dot(terms, features, precision=HIGH), "cells")
+        return jnp.sum(lax.all_gather(jnp.dot(terms, features, precision=HIGH), "cells"), axis=0)
 
     def total(packed):
         return lax.psum(packed, "feat")

time: 501 us -> 354 us (0.71)
  waiting for transfers between devices: 369 us -> 223 us
    psum x3 -> x0, waiting for transfers between devices: 314 us -> none  [collect(): return lax.psum(jnp.dot(terms, features, precision=HIGH), 'cells')]
    all_gather x0 -> x3, waiting for transfers between devices: none -> 169 us  [collect(): lax.all_gather(jnp.dot(terms, features, precision=HIGH), 'cells')]
where the time goes in v1:
time: 354 us
  waiting for transfers between devices  223 us (63%)
  matrix products  93.4 us (26%)
  between operations  18.2 us (5%)
  blocking collectives  9.52 us (3%)
  other arithmetic  9.12 us (3%)
    all_gather x3, waiting for transfers between devices, collect(): lax.all_gather(jnp.dot(terms, features, precision=HIGH), 'cells')  169 us
    dot_general x3, matrix products, row_sums(): lax.dot_general(coeffs, features, (((1,), (1,)), ((), ())), precision=HIG...  55.1 us
    psum x3, waiting for transfers between devices, row_sums(): summed = lax.psum(local_rows, 'feat')  53.9 us
    dot_general x3, matrix products, collect(): jnp.dot(terms, features, precision=HIGH)  38.3 us
    psum x3, blocking collectives, total(): return lax.psum(packed, 'feat')  9.52 us
  transfers between devices with their start and end apart: 6, of which 6 were waited for; matrix products, arithmetic and copies ran while one was open for 0% of the time, Pallas kernels for 0%

profile of v1, /device:TPU:0, one launch (start us, length us, event | category | flops | bytes accessed | tf_op | source)
XLA Modules:
  0.0 353.7 jit_solution(5152977687732616689)
XLA Ops:
  7.2 0.0 all-reduce.5.cloned.1.call-start
  7.2 19.7 %fusion.21 = f32[8,2048]{1,0:T(8,128)} fusion(f32[8,2048]{1,0:T(8,128)} %param.5, f32[2048,2048]{1,0:T(8,128)} %param.3), kind=kOutput, calls=%fused_computation.35 | convolution fusion | flops 402653184 | bytes 16908288 | tf_op jit(solution)/shard_map/dot_general | solution.py:17
  26.9 0.0 all-reduce.5.cloned.1.call-update
  27.0 0.0 all-gather.7.cloned.1.call-start
  27.0 20.5 %all-reduce.5.cloned.1.call-done = f32[8,2048]{1,0:T(8,128)} async-done(((f32[8,2048]{1,0:T(8,128)}), f32[8,2048]{1,0:T(8,128)}) %all-reduce.5.cloned.1.call-update) | async-done | bytes 65552 | tf_op jit(solution)/shard_map/psum | solution.py:24
  47.6 0.9 exponential_reduce_fusion
  48.5 14.2 %fusion.6 = f32[8,2048]{1,0:T(8,128)} fusion(f32[2048,2048]{1,0:T(8,128)} %param.3, s32[2048]{0:T(1024)S(1)} %copy-done.4, f32[8,2048]{1,0:T(8,128)} %all-reduce.5.cloned.1.call-done, f32[2048]{0:T(1024)S(1)} %exponential_reduce_fusion), kind=kOutput, calls=%fused_computation.19 | convolution fusion | flops 402718720 | bytes 16924672 | tf_op jit(solution)/shard_map/dot_general | solution.py:28
  62.6 0.2 all-reduce.7.cloned.1.call-start
  62.9 56.2 %all-gather.7.cloned.1.call-done = f32[128,2048]{1,0:T(8,128)} async-done(((f32[8,2048]{1,0:T(8,128)}), f32[128,2048]{1,0:T(8,128)}) %all-gather.7.cloned.1.call-update) | async-done | bytes 1048592 | tf_op jit(solution)/shard_map/all_gather | solution.py:28
  119.1 1.3 bitcast_reduce_fusion.2
  120.4 17.7 %fusion.9 = f32[8,2048]{1,0:T(8,128)} fusion(f32[2048,2048]{1,0:T(8,128)} %param.3, f32[8,2048]{1,0:T(8,128)S(1)} %multiply_add_fusion.2), kind=kOutput, calls=%fused_computation.25 | convolution fusion | flops 402669568 | bytes 16908288 | tf_op jit(solution)/shard_map/dot_general | solution.py:17
  138.1 0.0 all-gather.9.cloned.1.call-start
  138.1 16.7 %all-reduce.7.cloned.1.call-done = f32[8,2048]{1,0:T(8,128)} async-done(((f32[8,2048]{1,0:T(8,128)}), f32[8,2048]{1,0:T(8,128)}) %all-reduce.7.cloned.1.call-update) | async-done | bytes 65552 | tf_op jit(solution)/shard_map/psum | solution.py:24
  154.8 0.9 fusion.18
  155.7 12.1 %fusion.3 = f32[8,2048]{1,0:T(8,128)} fusion(f32[2048,2048]{1,0:T(8,128)} %param.3, f32[2048]{0:T(1024)S(1)} %fusion.18, f32[8,2048]{1,0:T(8,128)S(1)} %copy-done, f32[2048]{0:T(1024)S(1)} %exponential_reduce_fusion, f32[8,2048]{1,0:T(8,128)} %all-reduce.7.cloned.1.call-done), kind=kOutput, calls=%fused_computation.14 | convolution fusion | flops 402718720 | bytes 16990208 | tf_op jit(solution)/shard_map/dot_general | solution.py:28
  167.8 0.0 all-reduce.9.cloned.1.call-start
  167.9 56.4 %all-gather.9.cloned.1.call-done = f32[128,2048]{1,0:T(8,128)} async-done(((f32[8,2048]{1,0:T(8,128)}), f32[128,2048]{1,0:T(8,128)}) %all-gather.9.cloned.1.call-update) | async-done | bytes 1048592 | tf_op jit(solution)/shard_map/all_gather | solution.py:28
  224.3 1.3 bitcast_reduce_fusion.1
  225.5 0.6 multiply_reduce_fusion.2
  226.2 3.1 all-reduce
  230.6 0.6 multiply_reduce_fusion.1
  231.2 3.4 psum.53
  235.9 17.7 %fusion.14 = f32[8,2048]{1,0:T(8,128)} fusion(f32[2048,2048]{1,0:T(8,128)} %param.3, f32[8,2048]{1,0:T(8,128)S(1)} %multiply_add_fusion.2, f32[8,2048]{1,0:T(8,128)S(1)} %bitcast_reduce_fusion.1, f32[]{:T(128)S(6)} %div.31, f32[]{:T(128)S(6)} %div.30), kind=kOutput, calls=%fused_computation.30 | convolution fusion | flops 402784256 | bytes 16973832 | tf_op jit(solution)/shard_map/dot_general | solution.py:17
  253.6 0.0 all-gather.11.cloned.1.call-start
  253.7 16.7 %all-reduce.9.cloned.1.call-done = f32[8,2048]{1,0:T(8,128)} async-done(((f32[8,2048]{1,0:T(8,128)}), f32[8,2048]{1,0:T(8,128)}) %all-reduce.9.cloned.1.call-update) | async-done | bytes 65552 | tf_op jit(solution)/shard_map/psum | solution.py:24
  270.3 0.9 fusion.20
  271.3 12.1 %fusion = f32[8,2048]{1,0:T(8,128)} fusion(f32[2048,2048]{1,0:T(8,128)} %param.3, f32[2048]{0:T(1024)S(1)} %fusion.20, f32[8,2048]{1,0:T(8,128)S(1)} %copy-done, f32[2048]{0:T(1024)S(1)} %exponential_reduce_fusion, f32[8,2048]{1,0:T(8,128)} %all-reduce.9.cloned.1.call-done), kind=kOutput, calls=%fused_computation.6 | convolution fusion | flops 402718720 | bytes 16990208 | tf_op jit(solution)/shard_map/dot_general | solution.py:28
  283.4 56.5 %all-gather.11.cloned.1.call-done = f32[128,2048]{1,0:T(8,128)} async-done(((f32[8,2048]{1,0:T(8,128)}), f32[128,2048]{1,0:T(8,128)}) %all-gather.11.cloned.1.call-update) | async-done | bytes 1048592 | tf_op jit(solution)/shard_map/all_gather | solution.py:28
  339.9 1.3 bitcast_reduce_fusion
  341.1 0.6 multiply_reduce_fusion
  341.8 3.1 psum.55
  346.2 0.7 add_add_fusion
  (16 shorter events, 0.1 us)
Async XLA Ops:
  7.2 113.2 %copy-start.1 = (f32[8,2048]{1,0:T(8,128)S(1)}, f32[8,2048]{1,0:T(8,128)}, u32[]{:S(2)}) copy-start(f32[8,2048]{1,0:T(8,128)} %param.5) | copy-start | bytes 196612
  7.2 41.3 %copy-start.4 = (s32[2048]{0:T(1024)S(1)}, s32[2048]{0:T(1024)}, u32[]{:S(2)}) copy-start(s32[2048]{0:T(1024)} %param.4) | copy-start | bytes 24580
  7.2 40.4 %all-reduce.5.cloned.1.call-start = ((), (), s32[]{:S(2)}) async-start(), calls=%async_computation | async-start | bytes 131072 | tf_op jit(solution)/shard_map/psum | solution.py:24
  27.0 92.1 %all-gather.7.cloned.1.call-start = ((), (), s32[]{:S(2)}) async-start(), calls=%async_computation.3 | async-start | bytes 1114112 | tf_op jit(solution)/shard_map/all_gather | solution.py:28
  48.4 106.4 %copy-start = (f32[8,2048]{1,0:T(8,128)S(1)}, f32[8,2048]{1,0:T(8,128)}, u32[]{:S(2)}) copy-start(f32[8,2048]{1,0:T(8,128)} %all-reduce.5.cloned.1.call-done) | copy-start | bytes 196612
  62.6 92.2 %all-reduce.7.cloned.1.call-start = ((), (), s32[]{:S(2)}) async-start(), calls=%async_computation.1 | async-start | bytes 131072 | tf_op jit(solution)/shard_map/psum | solution.py:24
  138.1 86.2 %all-gather.9.cloned.1.call-start = ((), (), s32[]{:S(2)}) async-start(), calls=%async_computation.4 | async-start | bytes 1114112 | tf_op jit(solution)/shard_map/all_gather | solution.py:28
  167.8 102.5 %all-reduce.9.cloned.1.call-start = ((), (), s32[]{:S(2)}) async-start(), calls=%async_computation.2 | async-start | bytes 131072 | tf_op jit(solution)/shard_map/psum | solution.py:24
  235.9 110.3 %copy-start.2 = (f32[8,2048]{1,0:T(8,128)S(1)}, f32[8,2048]{1,0:T(8,128)}, u32[]{:S(2)}) copy-start(f32[8,2048]{1,0:T(8,128)} %all-reduce.7.cloned.1.call-done) | copy-start | bytes 196612
  253.6 86.2 %all-gather.11.cloned.1.call-start = ((), (), s32[]{:S(2)}) async-start(), calls=%async_computation.5 | async-start | bytes 1114112 | tf_op jit(solution)/shard_map/all_gather | solution.py:28
  270.3 75.8 %copy-start.3 = (f32[8,2048]{1,0:T(8,128)S(1)}, f32[8,2048]{1,0:T(8,128)}, u32[]{:S(2)}) copy-start(f32[8,2048]{1,0:T(8,128)} %all-reduce.9.cloned.1.call-done) | copy-start | bytes 196612
Sparse Core Ops, SparseCore 0:
  27.1 20.4 all-reduce.4
  62.8 56.2 all-gather.6
  138.2 16.5 all-reduce.6
  167.9 56.2 all-gather.8
  253.8 16.5 all-reduce.8
  283.5 56.2 all-gather.10
